TPU v7x, 32 devices: a whole 2x2x4 slice. The times are simulated.
32 devices in a mesh: groups: 2 (over y), seq: 4 (over z), fsdp: 4 (over x, core).
Axes of the slice: x: 2, y: 2, z: 4, core: 2. Of those that a mesh axis runs over, the one named last changes fastest.
Arguments:
- tokens: bfloat16 [1024, 1024], P(('groups', 'seq')), parts along dimension 0, may hold values from -16 to 16
- qkv_weight: bfloat16 [1024, 1536], P('seq', 'fsdp'), may hold values from -0.125 to 0.125
- covisible: int32 [8, 4], P('groups'), parts along dimension 0, may hold values 0 or 1
- block_drive: int32 [8], P('groups'), parts along dimension 0, may hold values from 0 to 2
- grad_out: bfloat16 [1024, 512], P(('groups', 'seq'), 'fsdp'), parts along dimension 0, may hold values from -6 to 6
Outputs:
- attention: bfloat16 [1024, 512], P(('groups', 'seq'), 'fsdp'), parts along dimension 0
- grad_input: bfloat16 [1024, 1024], P(('groups', 'seq'), 'fsdp'), parts along dimension 0
- grad_weight: float32 [2048, 1536], P(('groups', 'seq'), 'fsdp'), parts along dimension 0
There are 2 independent parts, one for each index of `groups`. A program takes and returns all parts, laid end to end along the dimension named above; an argument that names none is the same for every part. Nothing has to cross between parts.
All inputs are finite; a program needn't handle non-finite values.
Results may differ from a plain program's by a relative error of at most 0.018.
The roundings to bfloat16 on the way count: a program that leaves them out, or rounds other values in their place, can miss the bound.
Values may be sent and summed in bfloat16 or wider, within the bound.
No kernel may reach another device: no remote copies, remote signals or barrier semaphores. Data moves between devices by JAX's collectives and lax.ppermute only.
A program may use at most 64 MiB of HBM per device.

v0:
```python
import jax
import jax.numpy as jnp
from jax import lax
from jax.sharding import PartitionSpec as P

HD = 64
BLOCK = 128
MASKED_SCORE = -1e30


def query_visible(covisible, block_drive, first_block, block_count):
    own_rows = lax.dynamic_slice_in_dim(covisible, first_block, block_count, 0)
    own_drive = lax.dynamic_slice_in_dim(block_drive, first_block, block_count, 0)
    joined = jnp.logical_or(own_rows == 1, own_drive[:, None] == block_drive[None, :])
    return joined.astype(jnp.float32)


def key_visible(covisible, block_drive, first_block, block_count):
    own_columns = lax.dynamic_slice_in_dim(covisible, first_block, block_count, 1)
    own_drive = lax.dynamic_slice_in_dim(block_drive, first_block, block_count, 0)
    joined = jnp.logical_or(own_columns == 1, block_drive[:, None] == own_drive[None, :])
    return joined.astype(jnp.float32)


def block_onehot(length, block_total):
    member = lax.iota(jnp.int32, length) // BLOCK
    return (member[:, None] == lax.iota(jnp.int32, block_total)[None, :]).astype(jnp.float32)


def per_device(tokens, qkv_weight, covisible, block_drive, grad_out):
    local_rows = tokens.shape[0]
    seq_count = lax.axis_size("seq")
    seq_index = lax.axis_index("seq")
    out_width = qkv_weight.shape[1]
    local_heads = out_width // (3 * HD)
    block_count = local_rows // BLOCK
    block_total = covisible.shape[0]
    first_block = seq_index * block_count
    scaling = HD ** (-0.5)
    rows_visible = query_visible(covisible, block_drive, first_block, block_count)
    columns_visible = key_visible(covisible, block_drive, first_block, block_count)
    inputs = tokens
    projected = jnp.dot(
        inputs,
        lax.all_gather(qkv_weight, "seq", axis=0, tiled=True),
        preferred_element_type=jnp.float32,
    )
    projected = projected.astype(jnp.bfloat16).reshape(local_rows, local_heads, 3, HD)
    queries = projected[:, :, 0, :]
    local_keys = projected[:, :, 1, :]
    local_values = projected[:, :, 2, :]
    key_value = projected[:, :, 1:, :].reshape(local_rows, local_heads * 2 * HD)

    def local_visible(length):
        onehot = block_onehot(length, block_total)
        return (jnp.repeat(jnp.dot(rows_visible, onehot.T), BLOCK, axis=0) > 0.5)[None]

    panel = lax.all_gather(key_value, "seq", axis=0, tiled=True)
    running_max = jnp.full((local_heads, local_rows), MASKED_SCORE, jnp.float32)
    length = panel.shape[0]
    visible = local_visible(length)
    split_panel = panel.reshape(length, local_heads, 2, HD)
    scores = (
        jnp.einsum(
            "qhd,khd->hqk", queries, split_panel[:, :, 0, :], preferred_element_type=jnp.float32
        )
        * scaling
    )
    new_max = jnp.maximum(running_max, jnp.where(visible, scores, MASKED_SCORE).max(axis=2))
    shifted = jnp.exp(jnp.where(visible, scores - new_max[:, :, None], MASKED_SCORE))
    running_sum = shifted.sum(axis=2)
    wide_values = split_panel[:, :, 1, :].astype(jnp.float32)
    weighted = jnp.einsum(
        "hqk,khd->hqd",
        shifted,
        wide_values,
        precision=lax.Precision.HIGHEST,
        preferred_element_type=jnp.float32,
    )
    running_max, running_sum, weighted = (new_max, running_sum, weighted)
    attention_heads = (weighted / running_sum[:, :, None]).astype(jnp.bfloat16)
    attention = jnp.transpose(attention_heads, (1, 0, 2)).reshape(local_rows, local_heads * HD)
    log_total = running_max + jnp.log(running_sum)
    grad_heads = grad_out.reshape(local_rows, local_heads, HD)
    grad_dot_rows = jnp.sum(
        grad_heads.astype(jnp.float32)
        * attention.reshape(local_rows, local_heads, HD).astype(jnp.float32),
        axis=2,
    )
    grad_dot = jnp.transpose(grad_dot_rows)
    log_total_rows = jnp.transpose(log_total)
    all_log_total, all_grad_dot = (
        lax.all_gather(log_total_rows, "seq", axis=0, tiled=True),
        lax.all_gather(grad_dot_rows, "seq", axis=0, tiled=True),
    )
    query_rows = queries.reshape(local_rows, local_heads * HD)
    far_queries = lax.all_gather(query_rows, "seq", axis=0, tiled=True)
    far_grads = lax.all_gather(grad_out, "seq", axis=0, tiled=True)
    length = far_queries.shape[0]
    onehot = block_onehot(length, block_total)
    visible = (jnp.repeat(jnp.dot(onehot, columns_visible), BLOCK, axis=1) > 0.5)[None]
    far_heads = far_queries.reshape(length, local_heads, HD)
    far_grad_heads = far_grads.reshape(length, local_heads, HD)
    far_log_total = jnp.transpose(all_log_total)
    far_grad_dot = jnp.transpose(all_grad_dot)
    scores = (
        jnp.einsum("qhd,khd->hqk", far_heads, local_keys, preferred_element_type=jnp.float32)
        * scaling
    )
    probabilities = jnp.exp(jnp.where(visible, scores - far_log_total[:, :, None], MASKED_SCORE))
    grad_prob = jnp.einsum(
        "qhd,khd->hqk", far_grad_heads, local_values, preferred_element_type=jnp.float32
    )
    grad_score = (probabilities * (grad_prob - far_grad_dot[:, :, None]) * scaling).astype(
        jnp.bfloat16
    )
    grad_keys = jnp.einsum(
        "hqk,qhd->khd", grad_score, far_heads, preferred_element_type=jnp.float32
    )
    grad_values = jnp.einsum(
        "hqk,qhd->khd",
        probabilities.astype(jnp.bfloat16),
        far_grad_heads,
        preferred_element_type=jnp.float32,
    )
    grad_keys, grad_values = (grad_keys, grad_values)
    panel = lax.all_gather(key_value, "seq", axis=0, tiled=True)
    length = panel.shape[0]
    visible = local_visible(length)
    split_panel = panel.reshape(length, local_heads, 2, HD)
    panel_keys = split_panel[:, :, 0, :]
    scores = (
        jnp.einsum("qhd,khd->hqk", queries, panel_keys, preferred_element_type=jnp.float32)
        * scaling
    )
    probabilities = jnp.exp(jnp.where(visible, scores - log_total[:, :, None], MASKED_SCORE))
    grad_prob = jnp.einsum(
        "qhd,khd->hqk", grad_heads, split_panel[:, :, 1, :], preferred_element_type=jnp.float32
    )
    grad_score = (probabilities * (grad_prob - grad_dot[:, :, None]) * scaling).astype(jnp.bfloat16)
    grad_queries = jnp.einsum(
        "hqk,khd->qhd", grad_score, panel_keys, preferred_element_type=jnp.float32
    )
    grad_qkv = (
        jnp.stack([grad_queries, grad_keys, grad_values], axis=2)
        .astype(jnp.bfloat16)
        .reshape(local_rows, out_width)
    )
    partial_input = lax.dot_general(
        grad_qkv,
        lax.all_gather(qkv_weight, "seq", axis=0, tiled=True),
        (((1,), (1,)), ((), ())),
        preferred_element_type=jnp.float32,
    )
    grad_input = lax.psum_scatter(partial_input, "fsdp", scatter_dimension=1, tiled=True).astype(
        jnp.bfloat16
    )
    token_scale = (local_rows * seq_count) ** (-0.5)
    column_tokens = lax.all_to_all(tokens, "seq", split_axis=1, concat_axis=0, tiled=True)
    inputs = column_tokens
    summed_rows = lax.dot_general(
        inputs,
        lax.all_gather(grad_qkv, "seq", axis=0, tiled=True),
        (((0,), (0,)), ((), ())),
        preferred_element_type=jnp.float32,
    )
    grad_weight = summed_rows * token_scale
    return (attention, grad_input, grad_weight)


def solution(mesh):
    in_specs = (
        P(("groups", "seq"), None),
        P("seq", "fsdp"),
        P("groups", None),
        P("groups"),
        P(("groups", "seq"), "fsdp"),
    )
    out_specs = (
        P(("groups", "seq"), "fsdp"),
        P(("groups", "seq"), "fsdp"),
        P(("groups", "seq"), "fsdp"),
    )
    return jax.shard_map(
        per_device, mesh=mesh, in_specs=in_specs, out_specs=out_specs, check_vma=False
    )
```

profile of v0, /device:TPU:0, one launch (start us, length us, event | category | flops | bytes accessed | tf_op | source)
XLA Modules:
  0.0 121.6 jit_solution(15169649852441177908)
XLA Ops:
  7.2 0.6 copy-done.3
  7.9 0.6 dynamic_slice.11
  8.6 0.9 fusion.35
  9.5 21.6 %all_gather.23 = bf16[1024,384]{1,0:T(8,128)(2,1)S(1)} all-gather(bf16[256,384]{1,0:T(8,128)(2,1)} %param.6), channel_id=1, replica_groups=mesh['groups'=2,'seq'=4,'fsdp'=4] {'seq'}, dimensions={0}, use_global_device_ids=true | all-gather | bytes 983040 | tf_op jit(solution)/shard_map/all_gather | solution.py:45
  31.1 0.3 convolution_convert_fusion
  31.4 0.1 copy.26
  31.6 12.8 %all_gather.24 = bf16[512,256]{0,1:T(8,128)(2,1)S(1)} all-gather(bf16[128,256]{0,1:T(8,128)(2,1)S(1)} %bitcast.145), channel_id=1, replica_groups=mesh['groups'=2,'seq'=4,'fsdp'=4] {'seq'}, dimensions={0}, use_global_device_ids=true | all-gather | bytes 327680 | tf_op jit(solution)/shard_map/all_gather | solution.py:58
  44.4 0.3 select_reduce_fusion
  44.7 0.2 fusion.24
  45.1 0.8 copy-done.1
  45.8 0.1 copy.30
  45.9 13.3 %all_gather.27 = bf16[512,128]{1,0:T(8,128)(2,1)S(1)} all-gather(bf16[128,128]{1,0:T(8,128)(2,1)S(1)} %copy-done.1), channel_id=1, replica_groups=mesh['groups'=2,'seq'=4,'fsdp'=4] {'seq'}, dimensions={0}, use_global_device_ids=true | all-gather | bytes 163840 | tf_op jit(solution)/shard_map/all_gather | solution.py:98
  59.3 8.2 %all_gather.26 = f32[512,2]{0,1:T(2,128)S(1)} all-gather(f32[128,2]{0,1:T(2,128)S(1)} %bitcast_add_fusion), channel_id=1, replica_groups=mesh['groups'=2,'seq'=4,'fsdp'=4] {'seq'}, dimensions={0}, use_global_device_ids=true | all-gather | bytes 5120 | tf_op jit(solution)/shard_map/all_gather | solution.py:93
  67.6 0.9 fusion.34
  68.5 12.3 %all_gather.25 = bf16[512,128]{0,1:T(8,128)(2,1)S(1)} all-gather(bf16[128,128]{0,1:T(8,128)(2,1)S(1)} %bitcast.146), channel_id=1, replica_groups=mesh['groups'=2,'seq'=4,'fsdp'=4] {'seq'}, dimensions={0}, use_global_device_ids=true | all-gather | bytes 163840 | tf_op jit(solution)/shard_map/all_gather | solution.py:97
  80.8 0.6 multiply_reduce_fusion
  81.3 8.0 %all_gather.28 = f32[512,2]{0,1:T(2,128)S(1)} all-gather(f32[128,2]{0,1:T(2,128)S(1)} %get-tuple-element.14), channel_id=1, replica_groups=mesh['groups'=2,'seq'=4,'fsdp'=4] {'seq'}, dimensions={0}, use_global_device_ids=true | all-gather | bytes 5120 | tf_op jit(solution)/shard_map/all_gather | solution.py:94
  89.4 0.1 copy.34
  89.5 0.4 fusion.6
  89.9 0.2 fusion.20
  90.1 0.4 fusion.19
  90.5 0.5 fusion.18
  91.0 1.2 fusion.62
  92.2 0.8 copy.37
  93.0 3.4 %all-to-all-start = ((bf16[128,4,256]{0,2,1:T(8,128)(2,1)}), bf16[128,4,256]{0,2,1:T(8,128)(2,1)S(1)}, u32[]{:S(2)}, u32[]{:S(2)}) async-start(bf16[128,4,256]{0,2,1:T(8,128)(2,1)} %bitcast.36), calls=%async_computation.1 | async-start | bytes 524288 | tf_op jit(solution)/shard_map/all_to_all | solution.py:159
  96.5 0.7 copy.39
  97.2 14.2 %all_gather.29 = bf16[512,384]{0,1:T(8,128)(2,1)S(1)} all-gather(bf16[128,384]{0,1:T(8,128)(2,1)S(1)} %bitcast.134), channel_id=1, replica_groups=mesh['groups'=2,'seq'=4,'fsdp'=4] {'seq'}, dimensions={0}, use_global_device_ids=true | all-gather | bytes 491520 | tf_op jit(solution)/shard_map/all_gather | solution.py:163
  111.4 0.1 copy.38
  111.6 0.3 fusion.11
  111.8 0.9 copy.40
  112.7 0.5 reduce-scatter.2.cloned.1.call-done
  113.2 1.5 %convert_element_type.44 = bf16[128,256]{1,0:T(8,128)(2,1)} convert(f32[128,256]{1,0:T(8,128)} %reduce-scatter.2.cloned.1.call-done) | non-fusion elementwise | flops 32768 | bytes 196608 | tf_op jit(solution)/shard_map/convert_element_type | solution.py:155
  (21 shorter events, 0.4 us)
Async XLA Ops:
  7.2 106.1 %reduce-scatter.2.cloned.1.call-start = ((), (), s32[]{:S(2)}) async-start(), calls=%async_computation.2 | async-start | bytes 655360 | tf_op jit(solution)/shard_map/reduce_scatter | solution.py:155
  7.2 0.7 copy-start.3
  7.9 0.7 copy-start.2
  9.5 21.6 %copy-start = (bf16[128,1024]{1,0:T(8,128)(2,1)S(1)}, bf16[128,1024]{1,0:T(8,128)(2,1)}, u32[]{:S(2)}) copy-start(bf16[128,1024]{1,0:T(8,128)(2,1)} %param.5) | copy-start | bytes 786436
  45.1 0.8 copy-start.1
  93.0 18.4 %all-to-all-start = ((bf16[128,4,256]{0,2,1:T(8,128)(2,1)}), bf16[128,4,256]{0,2,1:T(8,128)(2,1)S(1)}, u32[]{:S(2)}, u32[]{:S(2)}) async-start(bf16[128,4,256]{0,2,1:T(8,128)(2,1)} %bitcast.36), calls=%async_computation.1 | async-start | bytes 524288 | tf_op jit(solution)/shard_map/all_to_all | solution.py:159
Sparse Core Ops, SparseCore 0:
  92.3 20.8 reduce-scatter.1
where the time goes:
time: 122 us
  blocking collectives  90.5 us (74%)
  between operations  14.2 us (12%)
  matrix products  5.87 us (5%)
  local copies, waits for them, and re-layouts  5.24 us (4%)
  starting transfers between devices  3.44 us (3%)
  other arithmetic  1.84 us (2%)
    all_gather x1, blocking collectives, per_device(): lax.all_gather(qkv_weight, 'seq', axis=0, tiled=True)  21.6 us
    all_gather x1, blocking collectives, per_device(): lax.all_gather(grad_qkv, 'seq', axis=0, tiled=True)  14.2 us
    all_gather x1, blocking collectives, per_device(): far_grads = lax.all_gather(grad_out, 'seq', axis=0, tiled=True)  13.3 us
    all_gather x1, blocking collectives, per_device(): panel = lax.all_gather(key_value, 'seq', axis=0, tiled=True)  12.8 us
    all_gather x1, blocking collectives, per_device(): far_queries = lax.all_gather(query_rows, 'seq', axis=0, tiled=True)  12.3 us
    all_gather x1, blocking collectives, per_device(): lax.all_gather(log_total_rows, 'seq', axis=0, tiled=True)  8.22 us
    all_gather x1, blocking collectives, per_device(): lax.all_gather(grad_dot_rows, 'seq', axis=0, tiled=True)  8.03 us
    unnamed x13, local copies, waits for them, and re-layouts  4.19 us
  transfers between devices with their start and end apart: 2, of which 1 were waited for; matrix products, arithmetic and copies ran while one was open for 2% of the time, Pallas kernels for 0%

commit v1 on v0

--- a/solution.py
+++ b/solution.py
@@ -6,6 +6,28 @@
 HD = 64
 BLOCK = 128
 MASKED_SCORE = -1e30
+
+
+def joined_along(parts, dim):
+    dims = list(parts.shape[1:])
+    dims[dim] *= parts.shape[0]
+    return jnp.moveaxis(parts, 0, dim).reshape(dims)
+
+
+def doubled(array, axis):
+    peers = lax.axis_size(axis)
+    tiles = array[None]
+    for level in range(peers.bit_length() - 1):
+        bit = 1 << level
+        other = lax.ppermute(tiles, axis, [(i, i ^ bit) for i in range(peers)])
+        both = jnp.stack([tiles, other])
+        upper = lax.axis_index(axis) >> level & 1
+        tiles = jnp.where(upper == 0, both, both[::-1]).reshape(-1, *array.shape)
+    return tiles
+
+
+def doubled_up(array, axis, dim):
+    return joined_along(doubled(array, axis), dim)
 
 
 def query_visible(covisible, block_drive, first_block, block_count):
@@ -41,9 +63,7 @@
     columns_visible = key_visible(covisible, block_drive, first_block, block_count)
     inputs = tokens
     projected = jnp.dot(
-        inputs,
-        lax.all_gather(qkv_weight, "seq", axis=0, tiled=True),
-        preferred_element_type=jnp.float32,
+        inputs, doubled_up(qkv_weight, "seq", 0), preferred_element_type=jnp.float32
     )
     projected = projected.astype(jnp.bfloat16).reshape(local_rows, local_heads, 3, HD)
     queries = projected[:, :, 0, :]

time: 122 us -> 143 us (1.17)
  blocking collectives: 90.5 us -> 108 us
  starting transfers between devices: 3.44 us -> 5.79 us
  matrix products: 5.87 us -> 7.35 us
    all_gather x1, blocking collectives: 13.3 us -> 25.2 us  [per_device(): far_grads = lax.all_gather(grad_out, 'seq', axis=0, tiled=True)]
    all_to_all x0 -> x1, blocking collectives: none -> 9.59 us  [per_device(): lax.all_to_all(tokens, 'seq', split_axis=1, concat_axis=0, tiled=True)]
    ppermute x0 -> x2, starting transfers between devices: none -> 5.75 us  [doubled(): other = lax.ppermute(tiles, axis, [(i, i ^ bit) for i in range(peers)])]
    all_gather x1, blocking collectives: 21.6 us -> 17 us  [per_device(): lax.all_gather(qkv_weight, 'seq', axis=0, tiled=True)]
    all_to_all x1 -> x0, starting transfers between devices: 3.41 us -> none  [per_device(): lax.all_to_all(tokens, 'seq', split_axis=1, concat_axis=0, tiled=True)]
    all_gather x1, blocking collectives: 8.03 us -> 9.63 us  [per_device(): lax.all_gather(grad_dot_rows, 'seq', axis=0, tiled=True)]
    unnamed x13 -> x11, local copies, waits for them, and re-layouts: 4.19 us -> 2.81 us
  transfers between devices with their start and end apart: 2 -> 3, of which waited for: 1 -> 0; matrix products, arithmetic and copies ran while one was open for 2% -> 5% of each run, Pallas kernels for 0% -> 0%
where the time goes in v1:
time: 143 us
  blocking collectives  108 us (76%)
  between operations  14.2 us (10%)
  matrix products  7.35 us (5%)
  starting transfers between devices  5.79 us (4%)
  local copies, waits for them, and re-layouts  5.07 us (4%)
  other arithmetic  2.22 us (2%)
    all_gather x1, blocking collectives, per_device(): far_grads = lax.all_gather(grad_out, 'seq', axis=0, tiled=True)  25.2 us
    all_gather x1, blocking collectives, per_device(): lax.all_gather(qkv_weight, 'seq', axis=0, tiled=True)  17 us
    all_gather x1, blocking collectives, per_device(): panel = lax.all_gather(key_value, 'seq', axis=0, tiled=True)  13.5 us
    all_gather x1, blocking collectives, per_device(): lax.all_gather(grad_qkv, 'seq', axis=0, tiled=True)  13.3 us
    all_gather x1, blocking collectives, per_device(): far_queries = lax.all_gather(query_rows, 'seq', axis=0, tiled=True)  12.3 us
    all_gather x1, blocking collectives, per_device(): lax.all_gather(grad_dot_rows, 'seq', axis=0, tiled=True)  9.63 us
    all_to_all x1, blocking collectives, per_device(): lax.all_to_all(tokens, 'seq', split_axis=1, concat_axis=0, tiled=True)  9.59 us
    all_gather x1, blocking collectives, per_device(): lax.all_gather(log_total_rows, 'seq', axis=0, tiled=True)  7.56 us
  transfers between devices with their start and end apart: 3, of which 0 were waited for; matrix products, arithmetic and copies ran while one was open for 5% of the time, Pallas kernels for 0%

profile of v1, /device:TPU:0, one launch (start us, length us, event | category | flops | bytes accessed | tf_op | source)
XLA Modules:
  0.0 142.8 jit_solution(10685395292872830290)
XLA Ops:
  7.2 3.1 %collective-permute-start = (bf16[1,256,384]{2,1,0:T(8,128)(2,1)}, bf16[1,256,384]{2,1,0:T(8,128)(2,1)S(1)}, u32[]{:S(2)}, u32[]{:S(2)}) collective-permute-start(bf16[1,256,384]{2,1,0:T(8,128)(2,1)} %bitcast.150), channel_id=1, source_target_pairs={{0,4},{4,0},{8,12},{12,8},{1,5},{5,1},{9,13},{13,9},{2,6},{6,2},{1... | collective-permute-start | bytes 589832 | tf_op jit(solution)/shard_map/ppermute | solution.py:22
  10.3 1.2 dynamic_slice.11
  11.6 0.8 constant_dynamic-slice_fusion
  12.4 1.6 %fusion.37 = f32[1,512]{1,0:T(1,128)S(1)} fusion(s32[512]{0:T(512)S(1)} %add_select_fusion, s32[4]{0:T(128)} %param.8, s32[4,4]{1,0:T(4,128)} %param.7, s32[]{:T(128)S(6)} %select_n.49, s32[]{:T(128)} %bitcast), kind=kOutput, calls=%fused_computation.52 | convolution fusion | flops 6156 | bytes 5636 | tf_op jit(solution)/shard_map/dot_general | solution.py:76
  14.0 1.6 %fusion.36 = f32[1,512]{1,0:T(1,128)S(1)} fusion(s32[512]{0:T(512)S(1)} %add_select_fusion, s32[4]{0:T(128)} %param.8, s32[4,1]{0,1:T(1,128)S(1)} %copy.45, s32[]{:T(128)} %bitcast), kind=kOutput, calls=%fused_computation.51 | convolution fusion | flops 6156 | bytes 4132 | tf_op jit(solution)/shard_map/dot_general | solution.py:121
  15.7 2.7 %collective-permute-start.1 = (bf16[2,256,384]{2,1,0:T(8,128)(2,1)S(1)}, bf16[2,256,384]{2,1,0:T(8,128)(2,1)S(1)}, u32[]{:S(2)}, u32[]{:S(2)}) collective-permute-start(bf16[2,256,384]{2,1,0:T(8,128)(2,1)S(1)} %get-tuple-element.13), channel_id=1, source_target_pairs={{0,8},{4,12},{8,0},{12,4},{1,9},{5,13},{9,1},{13,5},{2,10},{6,14},... | collective-permute-start | bytes 1179656 | tf_op jit(solution)/shard_map/ppermute | solution.py:22
  18.5 25.2 %all_gather.25 = bf16[512,128]{1,0:T(8,128)(2,1)S(1)} all-gather(bf16[128,128]{1,0:T(8,128)(2,1)S(1)} %copy-done.2), channel_id=1, replica_groups=mesh['groups'=2,'seq'=4,'fsdp'=4] {'seq'}, dimensions={0}, use_global_device_ids=true | all-gather | bytes 163840 | tf_op jit(solution)/shard_map/all_gather | solution.py:118
  43.7 0.1 copy.33
  43.9 17.0 %all_gather.27 = bf16[1024,384]{1,0:T(8,128)(2,1)S(1)} all-gather(bf16[256,384]{1,0:T(8,128)(2,1)S(1)} %copy-done.1), channel_id=1, replica_groups=mesh['groups'=2,'seq'=4,'fsdp'=4] {'seq'}, dimensions={0}, use_global_device_ids=true | all-gather | bytes 983040 | tf_op jit(solution)/shard_map/all_gather | solution.py:171
  61.0 0.1 reverse_select_fusion
  61.2 0.8 copy-done
  61.9 0.4 convolution_convert_fusion
  62.4 13.5 %all_gather.22 = bf16[512,256]{0,1:T(8,128)(2,1)S(1)} all-gather(bf16[128,256]{0,1:T(8,128)(2,1)S(1)} %bitcast.163), channel_id=1, replica_groups=mesh['groups'=2,'seq'=4,'fsdp'=4] {'seq'}, dimensions={0}, use_global_device_ids=true | all-gather | bytes 327680 | tf_op jit(solution)/shard_map/all_gather | solution.py:78
  75.9 0.3 select_reduce_fusion
  76.2 0.2 fusion.24
  76.5 12.3 %all_gather.23 = bf16[512,128]{0,1:T(8,128)(2,1)S(1)} all-gather(bf16[128,128]{0,1:T(8,128)(2,1)S(1)} %bitcast.165), channel_id=1, replica_groups=mesh['groups'=2,'seq'=4,'fsdp'=4] {'seq'}, dimensions={0}, use_global_device_ids=true | all-gather | bytes 163840 | tf_op jit(solution)/shard_map/all_gather | solution.py:117
  88.8 7.6 %all_gather.24 = f32[512,2]{0,1:T(2,128)S(1)} all-gather(f32[128,2]{0,1:T(2,128)S(1)} %bitcast_add_fusion), channel_id=1, replica_groups=mesh['groups'=2,'seq'=4,'fsdp'=4] {'seq'}, dimensions={0}, use_global_device_ids=true | all-gather | bytes 5120 | tf_op jit(solution)/shard_map/all_gather | solution.py:113
  96.3 0.6 multiply_reduce_fusion
  96.9 9.6 %all_gather.26 = f32[512,2]{0,1:T(2,128)S(1)} all-gather(f32[128,2]{0,1:T(2,128)S(1)} %get-tuple-element.16), channel_id=1, replica_groups=mesh['groups'=2,'seq'=4,'fsdp'=4] {'seq'}, dimensions={0}, use_global_device_ids=true | all-gather | bytes 5120 | tf_op jit(solution)/shard_map/all_gather | solution.py:114
  106.5 0.4 fusion.6
  106.9 0.2 fusion.20
  107.1 0.4 fusion.19
  107.5 0.5 fusion.18
  108.0 1.2 fusion.64
  109.2 0.2 copy.36
  109.4 9.6 %all_to_all.19 = bf16[128,4,256]{0,2,1:T(8,128)(2,1)S(1)} all-to-all(bf16[128,4,256]{0,2,1:T(8,128)(2,1)S(1)} %bitcast.146), channel_id=1, replica_groups=mesh['groups'=2,'seq'=4,'fsdp'=4] {'seq'}, dimensions={1} | all-to-all | bytes 524288 | tf_op jit(solution)/shard_map/all_to_all | solution.py:179
  119.0 0.1 copy.37
  119.2 0.7 copy.38
  119.9 13.3 %all_gather.28 = bf16[512,384]{0,1:T(8,128)(2,1)S(1)} all-gather(bf16[128,384]{0,1:T(8,128)(2,1)S(1)} %bitcast.149), channel_id=1, replica_groups=mesh['groups'=2,'seq'=4,'fsdp'=4] {'seq'}, dimensions={0}, use_global_device_ids=true | all-gather | bytes 491520 | tf_op jit(solution)/shard_map/all_gather | solution.py:183
  133.2 0.3 fusion.11
  133.4 0.9 copy.39
  134.4 1.5 %convert_element_type.48 = bf16[128,256]{1,0:T(8,128)(2,1)} convert(f32[128,256]{1,0:T(8,128)} %reduce-scatter.2.cloned.1.call-done) | non-fusion elementwise | flops 32768 | bytes 196608 | tf_op jit(solution)/shard_map/convert_element_type | solution.py:175
  (25 shorter events, 0.6 us)
Async XLA Ops:
  7.2 8.4 %copy-start.1 = (bf16[256,384]{1,0:T(8,128)(2,1)S(1)}, bf16[256,384]{1,0:T(8,128)(2,1)}, u32[]{:S(2)}) copy-start(bf16[256,384]{1,0:T(8,128)(2,1)} %param.6) | copy-start | bytes 589828
  7.2 127.2 %reduce-scatter.2.cloned.1.call-start = ((), (), s32[]{:S(2)}) async-start(), calls=%async_computation.2 | async-start | bytes 655360 | tf_op jit(solution)/shard_map/reduce_scatter | solution.py:175
  7.2 8.3 %collective-permute-start = (bf16[1,256,384]{2,1,0:T(8,128)(2,1)}, bf16[1,256,384]{2,1,0:T(8,128)(2,1)S(1)}, u32[]{:S(2)}, u32[]{:S(2)}) collective-permute-start(bf16[1,256,384]{2,1,0:T(8,128)(2,1)} %bitcast.150), channel_id=1, source_target_pairs={{0,4},{4,0},{8,12},{12,8},{1,5},{5,1},{9,13},{13,9},{2,6},{6,2},{1... | collective-permute-start | bytes 589832 | tf_op jit(solution)/shard_map/ppermute | solution.py:22
  15.6 2.8 %copy-start.2 = (bf16[128,128]{1,0:T(8,128)(2,1)S(1)}, bf16[128,128]{1,0:T(8,128)(2,1)}, u32[]{:S(2)}) copy-start(bf16[128,128]{1,0:T(8,128)(2,1)} %param.9) | copy-start | bytes 98308
  15.7 45.1 %collective-permute-start.1 = (bf16[2,256,384]{2,1,0:T(8,128)(2,1)S(1)}, bf16[2,256,384]{2,1,0:T(8,128)(2,1)S(1)}, u32[]{:S(2)}, u32[]{:S(2)}) collective-permute-start(bf16[2,256,384]{2,1,0:T(8,128)(2,1)S(1)} %get-tuple-element.13), channel_id=1, source_target_pairs={{0,8},{4,12},{8,0},{12,4},{1,9},{5,13},{9,1},{13,5},{2,10},{6,14},... | collective-permute-start | bytes 1179656 | tf_op jit(solution)/shard_map/ppermute | solution.py:22
  61.0 1.0 copy-start
Sparse Core Ops, SparseCore 0:
  109.4 19.8 reduce-scatter.1
